TPU v7x, 256 devices: a whole 4x4x8 slice. The times are simulated.
256 devices in a mesh: dp: 2 (over x_hi), mx: 8 (over z), my: 16 (over x_lo, y, core).
Axes of the slice: x: 4 (x_hi: 2, x_lo: 2; x = x_hi * 2 + x_lo), y: 4, z: 8, core: 2. Of those that a mesh axis runs over, the one named last changes fastest.
Arguments:
- inputs: bfloat16 [2048, 6144], P(('dp', 'my'), 'mx'), may hold values from -6 to 6
- hidden_in: bfloat16 [2048, 24576], P(('dp', 'mx'), 'my'), may hold values from -6 to 6
- out_grad: bfloat16 [2048, 6144], P(('dp', 'my'), 'mx'), may hold values from -6 to 6
- up_weight: bfloat16 [6144, 24576], P('mx', 'my'), may hold values from -0.078125 to 0.078125
- down_weight: bfloat16 [24576, 6144], P('my', 'mx'), may hold values from -0.0390625 to 0.0390625
Outputs:
- inputs_grad: bfloat16 [2048, 6144], P(('dp', 'my'), 'mx')
- up_grad: bfloat16 [6144, 24576], P('mx', 'my')
- down_grad: bfloat16 [24576, 6144], P('my', 'mx')
All inputs are finite; a program needn't handle non-finite values.
Results may differ from a plain program's by a relative error of at most 0.0059.
Values may be sent and summed in bfloat16 or wider, within the bound.
No kernel may reach another device: no remote copies, remote signals or barrier semaphores. Data moves between devices by JAX's collectives and lax.ppermute only.
A program may use at most 64 MiB of HBM per device.

v0:
```python
import jax
import jax.numpy as jnp
from jax import lax
from jax.sharding import PartitionSpec as P


def gelu_value(value):
    return 0.5 * value * (1.0 + lax.erf(value * 0.7071067811865476))


def gelu_slope(value):
    return (
        0.5 * (1.0 + lax.erf(value * 0.7071067811865476))
        + value * jnp.exp(-0.5 * value * value) * 0.3989422804014327
    )


def per_device(inputs, hidden_in, out_grad, up_weight, down_weight):
    total_tokens = out_grad.shape[0] * lax.axis_size("my") * lax.axis_size("dp")
    grad_scale = 1.0 / jnp.sqrt(jnp.float32(total_tokens))
    pre_value = hidden_in.astype(jnp.float32)
    act_local = gelu_value(pre_value).astype(jnp.bfloat16)
    act_whole = lax.all_gather(act_local, "mx", axis=0, tiled=True)
    input_whole, grad_whole = (
        lax.all_gather(inputs, "my", axis=0, tiled=True),
        lax.all_gather(out_grad, "my", axis=0, tiled=True),
    )
    down_part = (
        jnp.einsum("tf,td->fd", act_whole, grad_whole, preferred_element_type=jnp.float32)
        * grad_scale
    )
    row_block = grad_whole
    act_grad = lax.psum_scatter(
        jnp.einsum("td,fd->tf", row_block, down_weight, preferred_element_type=jnp.float32),
        "mx",
        scatter_dimension=0,
        tiled=True,
    )
    pre_grad = (act_grad * gelu_slope(pre_value)).astype(jnp.bfloat16)
    pre_whole = lax.all_gather(pre_grad, "mx", axis=0, tiled=True)
    row_block = pre_whole
    inputs_grad = lax.psum_scatter(
        jnp.einsum("tf,df->td", row_block, up_weight, preferred_element_type=jnp.float32),
        "my",
        scatter_dimension=0,
        tiled=True,
    ).astype(jnp.bfloat16)
    up_part = (
        jnp.einsum("td,tf->df", input_whole, pre_whole, preferred_element_type=jnp.float32)
        * grad_scale
    )
    up_total, down_total = (
        lax.psum(up_part.astype(jnp.bfloat16), "dp").astype(jnp.float32),
        lax.psum(down_part.astype(jnp.bfloat16), "dp").astype(jnp.float32),
    )
    return (inputs_grad, up_total.astype(jnp.bfloat16), down_total.astype(jnp.bfloat16))


def solution(mesh):
    return jax.shard_map(
        per_device,
        mesh=mesh,
        in_specs=(
            P(("dp", "my"), "mx"),
            P(("dp", "mx"), "my"),
            P(("dp", "my"), "mx"),
            P("mx", "my"),
            P("my", "mx"),
        ),
        out_specs=(P(("dp", "my"), "mx"), P("mx", "my"), P("my", "mx")),
        check_vma=False,
    )
```

profile of v0, /device:TPU:4, one launch (start us, length us, event | category | flops | bytes accessed | tf_op | source)
XLA Modules:
  0.0 477.7 jit_solution(6515074767499462279)
XLA Ops:
  7.2 0.0 copy-start
  7.2 0.0 all-gather.5.cloned.1.call-start
  7.2 0.7 all-gather.5.cloned.1.call-update
  7.9 0.0 reduce-scatter.3.cloned.1.call-start
  8.0 40.1 %all-gather.5.cloned.1.call-done = bf16[1024,768]{1,0:T(8,128)(2,1)} async-done(((bf16[64,768]{1,0:T(8,128)(2,1)}), bf16[1024,768]{1,0:T(8,128)(2,1)}) %all-gather.5.cloned.1.call-update) | async-done | bytes 1572880 | tf_op jit(solution)/shard_map/all_gather | solution.py:26
  48.1 0.0 copy-done
  48.1 6.0 %fusion.10 = f32[1024,1536]{1,0:T(8,128)} fusion(bf16[1024,768]{1,0:T(8,128)(2,1)} %all-gather.5.cloned.1.call-done, bf16[1536,768]{1,0:T(8,128)(2,1)S(1)} %copy-done), kind=kOutput, calls=%fused_computation.17 | convolution fusion | flops 2415919104 | bytes 10223616 | tf_op jit(solution)/shard_map/td,fd->tf/dot_general | solution.py:34
  54.0 0.0 reduce-scatter.3.cloned.1.call-update
  54.1 0.0 all-gather.11.cloned.1.call-start
  54.1 75.5 %reduce-scatter.3.cloned.1.call-done = f32[128,1536]{1,0:T(8,128)} async-done(((f32[1024,1536]{1,0:T(8,128)}), f32[128,1536]{1,0:T(8,128)}) %reduce-scatter.3.cloned.1.call-update) | async-done | bytes 786448 | tf_op jit(solution)/shard_map/reduce_scatter | solution.py:33
  129.6 0.0 copy-done.1
  129.6 2.4 fusion.9
  132.0 0.0 all-gather.11.cloned.1.call-update
  132.0 0.0 all-gather.9.cloned.1.call-start
  132.1 0.5 all-gather.9.cloned.1.call-update
  132.6 0.0 all-gather.7.cloned.1.call-start
  132.7 0.5 all-gather.7.cloned.1.call-update
  133.2 0.0 all-reduce.3.cloned.1.call-start
  133.3 42.5 %all-gather.11.cloned.1.call-done = bf16[1024,1536]{1,0:T(8,128)(2,1)} async-done(((bf16[128,1536]{1,0:T(8,128)(2,1)}), bf16[1024,1536]{1,0:T(8,128)(2,1)}) %all-gather.11.cloned.1.call-update) | async-done | bytes 3145744 | tf_op jit(solution)/shard_map/all_gather | solution.py:23
  175.8 6.4 %multiply_convert_fusion = bf16[1536,768]{1,0:T(8,128)(2,1)} fusion(bf16[1024,1536]{1,0:T(8,128)(2,1)} %all-gather.11.cloned.1.call-done, bf16[1024,768]{1,0:T(8,128)(2,1)} %all-gather.5.cloned.1.call-done), kind=kOutput, calls=%fused_computation | convolution fusion | flops 2418278400 | bytes 7077888 | tf_op jit(solution)/shard_map/tf,td->fd/dot_general | solution.py:29
  182.2 29.2 %all-gather.9.cloned.1.call-done = bf16[1024,768]{1,0:T(8,128)(2,1)} async-done(((bf16[64,768]{1,0:T(8,128)(2,1)}), bf16[1024,768]{1,0:T(8,128)(2,1)}) %all-gather.9.cloned.1.call-update) | async-done | bytes 1572880 | tf_op jit(solution)/shard_map/all_gather | solution.py:25
  211.4 46.9 %all-gather.7.cloned.1.call-done = bf16[1024,1536]{1,0:T(8,128)(2,1)} async-done(((bf16[128,1536]{1,0:T(8,128)(2,1)}), bf16[1024,1536]{1,0:T(8,128)(2,1)}) %all-gather.7.cloned.1.call-update) | async-done | bytes 3145744 | tf_op jit(solution)/shard_map/all_gather | solution.py:40
  258.3 6.4 %fusion = bf16[768,1536]{0,1:T(8,128)(2,1)} fusion(bf16[1024,1536]{1,0:T(8,128)(2,1)} %all-gather.7.cloned.1.call-done, bf16[1024,768]{1,0:T(8,128)(2,1)} %all-gather.9.cloned.1.call-done), kind=kOutput, calls=%fused_computation.2 | convolution fusion | flops 2418278400 | bytes 7077888 | tf_op jit(solution)/shard_map/td,tf->df/dot_general | solution.py:49
  264.8 0.0 all-reduce.3.cloned.1.call-update
  264.8 0.0 reduce-scatter.5.cloned.1.call-start
  264.8 6.9 %fusion.11 = f32[1024,768]{1,0:T(8,128)} fusion(bf16[1024,1536]{1,0:T(8,128)(2,1)} %all-gather.7.cloned.1.call-done, bf16[768,1536]{1,0:T(8,128)(2,1)} %param.8), kind=kOutput, calls=%fused_computation.18 | convolution fusion | flops 2415919104 | bytes 8650752 | tf_op jit(solution)/shard_map/tf,df->td/dot_general | solution.py:43
  271.8 0.0 reduce-scatter.5.cloned.1.call-update
  271.8 121.6 %all-reduce.3.cloned.1.call-done = (bf16[768,1536]{0,1:T(8,128)(2,1)}, bf16[1536,768]{1,0:T(8,128)(2,1)}) async-done(((bf16[768,1536]{0,1:T(8,128)(2,1)}, bf16[1536,768]{1,0:T(8,128)(2,1)}), (bf16[768,1536]{0,1:T(8,128)(2,1)}, bf16[1536,768]{1,0:T(8,128)(2,1)})) %all-reduce.3.cloned.1.call-update) | async-done | bytes 4718608 | tf_op jit(solution)/shard_map/psum | solution.py:53
  393.4 4.3 copy.8
  397.7 68.3 %reduce-scatter.5.cloned.1.call-done = f32[64,768]{1,0:T(8,128)} async-done(((f32[1024,768]{1,0:T(8,128)}), f32[64,768]{1,0:T(8,128)}) %reduce-scatter.5.cloned.1.call-update) | async-done | bytes 196624 | tf_op jit(solution)/shard_map/reduce_scatter | solution.py:42
  466.0 1.6 convert_element_type.27
  467.6 3.2 copy.11
  (1 shorter events, 0.0 us)
Async XLA Ops:
  7.2 40.9 %copy-start = (bf16[1536,768]{1,0:T(8,128)(2,1)S(1)}, bf16[1536,768]{1,0:T(8,128)(2,1)}, u32[]{:S(2)}) copy-start(bf16[1536,768]{1,0:T(8,128)(2,1)} %param.9) | copy-start | bytes 7077892
  7.2 40.9 %all-gather.5.cloned.1.call-start = ((), (), s32[]{:S(2)}) async-start(), calls=%async_computation.2 | async-start | bytes 1671168 | tf_op jit(solution)/shard_map/all_gather | solution.py:26
  7.9 121.7 %reduce-scatter.3.cloned.1.call-start = ((), (), s32[]{:S(2)}) async-start(), calls=%async_computation.3 | async-start | bytes 7077888 | tf_op jit(solution)/shard_map/reduce_scatter | solution.py:33
  54.0 75.6 %copy-start.1 = (bf16[128,1536]{1,0:T(8,128)(2,1)S(1)}, bf16[128,1536]{1,0:T(8,128)(2,1)}, u32[]{:S(2)}) copy-start(bf16[128,1536]{1,0:T(8,128)(2,1)} %param.6) | copy-start | bytes 1179652
  54.1 121.8 %all-gather.11.cloned.1.call-start = ((), (), s32[]{:S(2)}) async-start(), calls=%async_computation.7 | async-start | bytes 3538944 | tf_op jit(solution)/shard_map/all_gather | solution.py:23
  132.0 79.4 %all-gather.9.cloned.1.call-start = ((), (), s32[]{:S(2)}) async-start(), calls=%async_computation.6 | async-start | bytes 1671168 | tf_op jit(solution)/shard_map/all_gather | solution.py:25
  132.6 125.7 %all-gather.7.cloned.1.call-start = ((), (), s32[]{:S(2)}) async-start(), calls=%async_computation.4 | async-start | bytes 3538944 | tf_op jit(solution)/shard_map/all_gather | solution.py:40
  133.2 260.2 %all-reduce.3.cloned.1.call-start = ((), (), s32[]{:S(2)}) async-start(), calls=%async_computation.8 | async-start | bytes 9437184 | tf_op jit(solution)/shard_map/psum | solution.py:53
  264.8 201.2 %reduce-scatter.5.cloned.1.call-start = ((), (), s32[]{:S(2)}) async-start(), calls=%async_computation.5 | async-start | bytes 3342336 | tf_op jit(solution)/shard_map/reduce_scatter | solution.py:42
Sparse Core Ops, SparseCore 0:
  9.8 38.1 all-gather.4
  54.2 75.3 reduce-scatter.2
  132.2 43.5 all-gather.10
  177.5 33.8 all-gather.8
  213.1 45.2 all-gather.6
  264.9 128.4 all-reduce.2
  396.0 70.0 reduce-scatter.4
where the time goes:
time: 478 us
  waiting for transfers between devices  426 us (89%)
  matrix products  25.8 us (5%)
  between operations  14.1 us (3%)
  local copies, waits for them, and re-layouts  7.51 us (2%)
    psum x1, waiting for transfers between devices, per_device(): lax.psum(up_part.astype(jnp.bfloat16), 'dp').astype(jnp.float32)  122 us
    reduce_scatter x1, waiting for transfers between devices, per_device(): lax.psum_scatter(jnp.einsum('td,fd->tf', row_block, down_weight, preferre...  75.5 us
    reduce_scatter x1, waiting for transfers between devices, per_device(): lax.psum_scatter(jnp.einsum('tf,df->td', row_block, up_weight, preferred_...  68.3 us
    all_gather x1, waiting for transfers between devices, per_device(): pre_whole = lax.all_gather(pre_grad, 'mx', axis=0, tiled=True)  46.9 us
    all_gather x1, waiting for transfers between devices, per_device(): act_whole = lax.all_gather(act_local, 'mx', axis=0, tiled=True)  42.5 us
    all_gather x1, waiting for transfers between devices, per_device(): lax.all_gather(out_grad, 'my', axis=0, tiled=True)  40.1 us
    all_gather x1, waiting for transfers between devices, per_device(): lax.all_gather(inputs, 'my', axis=0, tiled=True)  29.2 us
  transfers between devices with their start and end apart: 7, of which 7 were waited for; matrix products, arithmetic and copies ran while one was open for 4% of the time, Pallas kernels for 0%

commit v1 on v0

--- a/solution.py
+++ b/solution.py
@@ -22,7 +22,9 @@
     act_local = gelu_value(pre_value).astype(jnp.bfloat16)
     act_whole = lax.all_gather(act_local, "mx", axis=0, tiled=True)
     input_whole, grad_whole = (
-        lax.all_gather(inputs, "my", axis=0, tiled=True),
+        jnp.concatenate(
+            lax.all_to_all(jnp.stack([inputs] * lax.axis_size("my")), "my", 0, 0), axis=0
+        ),
         lax.all_gather(out_grad, "my", axis=0, tiled=True),
     )
     down_part = (

time: 478 us -> 441 us (0.923)
  waiting for transfers between devices: 426 us -> 382 us
  starting transfers between devices: 0.28 us -> 5.29 us
    all_gather x1 -> x0, waiting for transfers between devices: 29.2 us -> none  [per_device(): lax.all_gather(inputs, 'my', axis=0, tiled=True)]
    all_gather x1, waiting for transfers between devices: 46.9 us -> 38.9 us  [per_device(): pre_whole = lax.all_gather(pre_grad, 'mx', axis=0, tiled=True)]
    all_gather x1, waiting for transfers between devices: 42.5 us -> 36.8 us  [per_device(): act_whole = lax.all_gather(act_local, 'mx', axis=0, tiled=True)]
    all_to_all x0 -> x1, starting transfers between devices: none -> 5.05 us  [per_device(): lax.all_to_all(jnp.stack([inputs] * lax.axis_size('my')), 'my', 0, 0)]
  transfers between devices with their start and end apart: 7 -> 7, of which waited for: 7 -> 6; matrix products, arithmetic and copies ran while one was open for 4% -> 4% of each run, Pallas kernels for 0% -> 0%
where the time goes in v1:
time: 441 us; the launch traced here: 440 us
  waiting for transfers between devices  382 us (87%)
  matrix products  25.8 us (6%)
  between operations  14.1 us (3%)
  local copies, waits for them, and re-layouts  8.82 us (2%)
  starting transfers between devices  5.29 us (1%)
    psum x1, waiting for transfers between devices, per_device(): lax.psum(up_part.astype(jnp.bfloat16), 'dp').astype(jnp.float32)  122 us
    reduce_scatter x1, waiting for transfers between devices, per_device(): lax.psum_scatter(jnp.einsum('td,fd->tf', row_block, down_weight, preferre...  75.5 us
    reduce_scatter x1, waiting for transfers between devices, per_device(): lax.psum_scatter(jnp.einsum('tf,df->td', row_block, up_weight, preferred_...  68.2 us
    all_gather x1, waiting for transfers between devices, per_device(): lax.all_gather(out_grad, 'my', axis=0, tiled=True)  40.1 us
    all_gather x1, waiting for transfers between devices, per_device(): pre_whole = lax.all_gather(pre_grad, 'mx', axis=0, tiled=True)  38.9 us
    all_gather x1, waiting for transfers between devices, per_device(): act_whole = lax.all_gather(act_local, 'mx', axis=0, tiled=True)  36.8 us
  transfers between devices with their start and end apart: 7, of which 6 were waited for; matrix products, arithmetic and copies ran while one was open for 4% of the time, Pallas kernels for 0%

profile of v1, /device:TPU:4, one launch (start us, length us, event | category | flops | bytes accessed | tf_op | source)
XLA Modules:
  0.0 440.3 jit_solution(10240796397283746341)
XLA Ops:
  7.2 0.0 copy-start
  7.2 0.0 all-gather.4.cloned.1.call-start
  7.2 0.7 all-gather.4.cloned.1.call-update
  7.9 0.0 reduce-scatter.3.cloned.1.call-start
  8.0 40.1 %all-gather.4.cloned.1.call-done = bf16[1024,768]{1,0:T(8,128)(2,1)} async-done(((bf16[64,768]{1,0:T(8,128)(2,1)}), bf16[1024,768]{1,0:T(8,128)(2,1)}) %all-gather.4.cloned.1.call-update) | async-done | bytes 1572880 | tf_op jit(solution)/shard_map/all_gather | solution.py:28
  48.1 0.0 copy-done
  48.1 6.0 %fusion.10 = f32[1024,1536]{1,0:T(8,128)} fusion(bf16[1024,768]{1,0:T(8,128)(2,1)} %all-gather.4.cloned.1.call-done, bf16[1536,768]{1,0:T(8,128)(2,1)S(1)} %copy-done), kind=kOutput, calls=%fused_computation.17 | convolution fusion | flops 2415919104 | bytes 10223616 | tf_op jit(solution)/shard_map/td,fd->tf/dot_general | solution.py:36
  54.0 0.0 reduce-scatter.3.cloned.1.call-update
  54.1 0.0 copy-start.2
  54.1 0.0 all-gather.8.cloned.1.call-start
  54.1 75.5 %reduce-scatter.3.cloned.1.call-done = f32[128,1536]{1,0:T(8,128)} async-done(((f32[1024,1536]{1,0:T(8,128)}), f32[128,1536]{1,0:T(8,128)}) %reduce-scatter.3.cloned.1.call-update) | async-done | bytes 786448 | tf_op jit(solution)/shard_map/reduce_scatter | solution.py:35
  129.6 2.4 fusion.9
  132.0 0.0 all-gather.8.cloned.1.call-update
  132.0 0.0 all-gather.6.cloned.1.call-start
  132.1 0.5 all-gather.6.cloned.1.call-update
  132.6 1.3 stack.2
  133.9 5.0 %all-to-all-start = ((bf16[16,64,768]{2,1,0:T(8,128)(2,1)}), bf16[16,64,768]{2,1,0:T(8,128)(2,1)}, u32[]{:S(2)}, u32[]{:S(2)}) async-start(bf16[16,64,768]{2,1,0:T(8,128)(2,1)} %stack.2), calls=%async_computation.2 | async-start | bytes 3145728 | tf_op jit(solution)/shard_map/all_to_all | solution.py:26
  139.0 0.0 all-reduce.3.cloned.1.call-start
  139.0 36.8 %all-gather.8.cloned.1.call-done = bf16[1024,1536]{1,0:T(8,128)(2,1)} async-done(((bf16[128,1536]{1,0:T(8,128)(2,1)}), bf16[1024,1536]{1,0:T(8,128)(2,1)}) %all-gather.8.cloned.1.call-update) | async-done | bytes 3145744 | tf_op jit(solution)/shard_map/all_gather | solution.py:23
  175.8 6.4 %multiply_convert_fusion = bf16[1536,768]{1,0:T(8,128)(2,1)} fusion(bf16[1024,1536]{1,0:T(8,128)(2,1)} %all-gather.8.cloned.1.call-done, bf16[1024,768]{1,0:T(8,128)(2,1)} %all-gather.4.cloned.1.call-done), kind=kOutput, calls=%fused_computation | convolution fusion | flops 2418278400 | bytes 7077888 | tf_op jit(solution)/shard_map/tf,td->fd/dot_general | solution.py:31
  182.2 0.0 all-to-all-done
  182.2 38.9 %all-gather.6.cloned.1.call-done = bf16[1024,1536]{1,0:T(8,128)(2,1)} async-done(((bf16[128,1536]{1,0:T(8,128)(2,1)}), bf16[1024,1536]{1,0:T(8,128)(2,1)}) %all-gather.6.cloned.1.call-update) | async-done | bytes 3145744 | tf_op jit(solution)/shard_map/all_gather | solution.py:42
  221.1 6.4 %fusion = bf16[768,1536]{0,1:T(8,128)(2,1)} fusion(bf16[1024,1536]{1,0:T(8,128)(2,1)} %all-gather.6.cloned.1.call-done, bf16[1024,768]{1,0:T(8,128)(2,1)} %bitcast), kind=kOutput, calls=%fused_computation.2 | convolution fusion | flops 2418278400 | bytes 7077888 | tf_op jit(solution)/shard_map/td,tf->df/dot_general | solution.py:51
  227.5 0.0 all-reduce.3.cloned.1.call-update
  227.6 0.0 reduce-scatter.5.cloned.1.call-start
  227.6 6.9 %fusion.11 = f32[1024,768]{1,0:T(8,128)} fusion(bf16[1024,1536]{1,0:T(8,128)(2,1)} %all-gather.6.cloned.1.call-done, bf16[768,1536]{1,0:T(8,128)(2,1)} %param.8), kind=kOutput, calls=%fused_computation.18 | convolution fusion | flops 2415919104 | bytes 8650752 | tf_op jit(solution)/shard_map/tf,df->td/dot_general | solution.py:45
  234.5 0.0 reduce-scatter.5.cloned.1.call-update
  234.6 121.6 %all-reduce.3.cloned.1.call-done = (bf16[768,1536]{0,1:T(8,128)(2,1)}, bf16[1536,768]{1,0:T(8,128)(2,1)}) async-done(((bf16[768,1536]{0,1:T(8,128)(2,1)}, bf16[1536,768]{1,0:T(8,128)(2,1)}), (bf16[768,1536]{0,1:T(8,128)(2,1)}, bf16[1536,768]{1,0:T(8,128)(2,1)})) %all-reduce.3.cloned.1.call-update) | async-done | bytes 4718608 | tf_op jit(solution)/shard_map/psum | solution.py:55
  356.2 4.3 copy.8
  360.5 68.2 %reduce-scatter.5.cloned.1.call-done = f32[64,768]{1,0:T(8,128)} async-done(((f32[1024,768]{1,0:T(8,128)}), f32[64,768]{1,0:T(8,128)}) %reduce-scatter.5.cloned.1.call-update) | async-done | bytes 196624 | tf_op jit(solution)/shard_map/reduce_scatter | solution.py:44
  428.7 1.6 convert_element_type.27
  430.2 3.2 copy.11
  (3 shorter events, 0.0 us)
Async XLA Ops:
  7.2 40.9 %copy-start = (bf16[1536,768]{1,0:T(8,128)(2,1)S(1)}, bf16[1536,768]{1,0:T(8,128)(2,1)}, u32[]{:S(2)}) copy-start(bf16[1536,768]{1,0:T(8,128)(2,1)} %param.9) | copy-start | bytes 7077892
  7.2 40.9 %all-gather.4.cloned.1.call-start = ((), (), s32[]{:S(2)}) async-start(), calls=%async_computation.3 | async-start | bytes 1671168 | tf_op jit(solution)/shard_map/all_gather | solution.py:28
  7.9 121.7 %reduce-scatter.3.cloned.1.call-start = ((), (), s32[]{:S(2)}) async-start(), calls=%async_computation.4 | async-start | bytes 7077888 | tf_op jit(solution)/shard_map/reduce_scatter | solution.py:35
  54.0 75.6 %copy-start.1 = (bf16[128,1536]{1,0:T(8,128)(2,1)S(1)}, bf16[128,1536]{1,0:T(8,128)(2,1)}, u32[]{:S(2)}) copy-start(bf16[128,1536]{1,0:T(8,128)(2,1)} %param.6) | copy-start | bytes 1179652
  54.1 78.6 %copy-start.2 = (bf16[64,768]{1,0:T(8,128)(2,1)S(1)}, bf16[64,768]{1,0:T(8,128)(2,1)}, u32[]{:S(2)}) copy-start(bf16[64,768]{1,0:T(8,128)(2,1)} %param.5) | copy-start | bytes 294916
  54.1 121.7 %all-gather.8.cloned.1.call-start = ((), (), s32[]{:S(2)}) async-start(), calls=%async_computation.7 | async-start | bytes 3538944 | tf_op jit(solution)/shard_map/all_gather | solution.py:23
  132.0 89.1 %all-gather.6.cloned.1.call-start = ((), (), s32[]{:S(2)}) async-start(), calls=%async_computation.5 | async-start | bytes 3538944 | tf_op jit(solution)/shard_map/all_gather | solution.py:42
  133.9 48.3 %all-to-all-start = ((bf16[16,64,768]{2,1,0:T(8,128)(2,1)}), bf16[16,64,768]{2,1,0:T(8,128)(2,1)}, u32[]{:S(2)}, u32[]{:S(2)}) async-start(bf16[16,64,768]{2,1,0:T(8,128)(2,1)} %stack.2), calls=%async_computation.2 | async-start | bytes 3145728 | tf_op jit(solution)/shard_map/all_to_all | solution.py:26
  139.0 217.2 %all-reduce.3.cloned.1.call-start = ((), (), s32[]{:S(2)}) async-start(), calls=%async_computation.8 | async-start | bytes 9437184 | tf_op jit(solution)/shard_map/psum | solution.py:55
  227.6 201.1 %reduce-scatter.5.cloned.1.call-start = ((), (), s32[]{:S(2)}) async-start(), calls=%async_computation.6 | async-start | bytes 3342336 | tf_op jit(solution)/shard_map/reduce_scatter | solution.py:44
Sparse Core Ops, SparseCore 0:
  9.8 38.1 all-gather.3
  54.2 75.3 reduce-scatter.2
  132.2 43.5 all-gather.7
  177.5 43.5 all-gather.5
  227.7 128.4 all-reduce.2
  358.6 70.0 reduce-scatter.4
